TPU v7x, 32 devices: a whole 2x2x4 slice. The times are simulated.
32 devices in a mesh: gx: 8 (over y, x, core), gy: 4 (over z).
Axes of the slice: x: 2, y: 2, z: 4, core: 2. Of those that a mesh axis runs over, the one named last changes fastest.
Arguments:
- activations: bfloat16 [1024, 7168], P('gx', 'gy'), may hold values from -6 to 6
- out_grad: bfloat16 [1024, 7168], P('gx', 'gy'), may hold values from -0.59765625 to 0.59765625
- saved_gate: bfloat16 [1024, 2, 1024], P('gx', None, 'gy'), may hold values from -9 to 9
- saved_up: bfloat16 [1024, 2, 1024], P('gx', None, 'gy'), may hold values from -6 to 6
- route_ids: int32 [1024, 2], P('gx'), may hold values from 0 to 7, all different within a row; in each aligned block of 128 rows (0 to 127, 128 to 255, ...) at most 48 rows name the same one
- route_weight: float32 [1024, 2], P('gx'), may hold values from 0.1 to 1
- down_weight: bfloat16 [8, 1024, 7168], P('gx', None, 'gy'), may hold values from -0.1875 to 0.1875
Outputs:
- grad_gate: bfloat16 [8, 7168, 1024], P('gx', 'gy')
- grad_up: bfloat16 [8, 7168, 1024], P('gx', 'gy')
- grad_down: bfloat16 [8, 1024, 7168], P('gx', None, 'gy')
Inputs may be any that keep to these rules, and one draw needn't show every extreme that they name: `route_ids`: each token names 2 different experts. Within each aligned block of 128 tokens (one index of gx) no expert is named by more than 48 tokens, a bound that some block reaches.
All inputs are finite; a program needn't handle non-finite values.
Results may differ from a plain program's by a relative error of at most 0.02.
Values may be sent and summed in bfloat16 or wider, within the bound.
A program may use at most 64 MiB of HBM per device.

v0:
```python
import jax
import jax.numpy as jnp
from jax import lax
from jax.sharding import PartitionSpec as P

MOST = 48


def local_grads(hidden_grad, gate_rows, up_rows):
    gate_val = gate_rows.astype(jnp.float32)
    up_val = up_rows.astype(jnp.float32)
    gate_sig = jax.nn.sigmoid(gate_val)
    silu_val = gate_val * gate_sig
    hidden_act = (silu_val * up_val).astype(jnp.bfloat16)
    grad_upper = (hidden_grad * silu_val).astype(jnp.bfloat16)
    grad_gated = (hidden_grad * up_val * gate_sig * (1.0 + gate_val * (1.0 - gate_sig))).astype(
        jnp.bfloat16
    )
    return (hidden_act, grad_gated, grad_upper)


def contract_rows(left, right):
    return lax.dot_general(
        left, right, (((0,), (0,)), ((), ())), preferred_element_type=jnp.float32
    ).astype(jnp.bfloat16)


def slot_rows(route_ids, experts):
    flat_ids = route_ids.reshape(-1)
    onehot = (flat_ids[:, None] == jnp.arange(experts, dtype=jnp.int32)[None, :]).astype(jnp.int32)
    rank_in = jnp.sum((jnp.cumsum(onehot, axis=0) - onehot) * onehot, axis=1)
    return flat_ids * MOST + rank_in


def pack_rows(values, target, experts):
    buffer = jnp.zeros((experts * MOST, values.shape[-1]), values.dtype).at[target].set(values)
    return buffer.reshape(experts, MOST, values.shape[-1])


def merge_rows(values):
    return values.reshape(-1, values.shape[-1])


def on_device(activations, out_grad, saved_gate, saved_up, route_ids, route_weight, down_weight):
    experts = lax.axis_size("gx")
    top_count = route_ids.shape[1]
    target = slot_rows(route_ids, experts)
    act_routes = pack_rows(jnp.repeat(activations, top_count, axis=0), target, experts)
    scaled = (
        route_weight.reshape(-1, 1) * jnp.repeat(out_grad, top_count, axis=0).astype(jnp.float32)
    ).astype(jnp.bfloat16)
    grad_routes = pack_rows(scaled, target, experts)
    gate_routes = pack_rows(saved_gate.reshape(-1, saved_gate.shape[-1]), target, experts)
    up_routes = pack_rows(saved_up.reshape(-1, saved_up.shape[-1]), target, experts)
    rows_act, rows_grad, gate_rows, up_rows = (
        lax.all_to_all(act_routes, "gx", split_axis=0, concat_axis=0, tiled=True),
        lax.all_to_all(grad_routes, "gx", split_axis=0, concat_axis=0, tiled=True),
        lax.all_to_all(gate_routes, "gx", split_axis=0, concat_axis=0, tiled=True),
        lax.all_to_all(up_routes, "gx", split_axis=0, concat_axis=0, tiled=True),
    )
    rows_grad = merge_rows(rows_grad)
    gate_rows = merge_rows(gate_rows)
    up_rows = merge_rows(up_rows)
    weight = down_weight[0]
    partial_value = lax.dot_general(
        rows_grad, weight, (((1,), (1,)), ((), ())), preferred_element_type=jnp.float32
    )
    rows_act = merge_rows(rows_act)
    hidden_grad = lax.psum(partial_value.astype(jnp.bfloat16), "gy").astype(jnp.float32)
    gate_full, up_full = (
        lax.all_gather(gate_rows, "gy", axis=1, tiled=True),
        lax.all_gather(up_rows, "gy", axis=1, tiled=True),
    )
    hidden_act, grad_gated, grad_upper = local_grads(hidden_grad, gate_full, up_full)
    grad_gate = contract_rows(rows_act, grad_gated)[None]
    grad_up = contract_rows(rows_act, grad_upper)[None]
    grad_down = contract_rows(hidden_act, rows_grad)[None]
    return (grad_gate, grad_up, grad_down)


def solution(mesh):
    placed = (
        P("gx", "gy"),
        P("gx", "gy"),
        P("gx", None, "gy"),
        P("gx", None, "gy"),
        P("gx", None),
        P("gx", None),
        P("gx", None, "gy"),
    )
    return jax.shard_map(
        on_device,
        mesh=mesh,
        in_specs=placed,
        out_specs=(P("gx", "gy", None), P("gx", "gy", None), P("gx", None, "gy")),
        check_vma=False,
    )
```

profile of v0, /device:TPU:0, one launch (start us, length us, event | category | flops | bytes accessed | tf_op | source)
XLA Modules:
  0.0 144.9 jit_solution(7677745777979854261)
XLA Ops:
  7.2 0.0 copy-start.3
  7.2 0.0 copy-start.1
  7.2 0.7 broadcast_multiply_fusion
  7.9 0.8 copy.11
  8.7 0.1 eq.29
  8.8 0.1 eq.25
  9.0 0.1 copy.10
  9.1 0.1 mul.52
  9.3 0.6 reduce-window.6
  9.8 0.2 slice_reduce_fusion
  10.1 1.0 reshape.129
  11.1 0.1 fusion.31
  11.2 2.1 %scatter_custom_fusion.3 = bf16[384,256]{1,0:T(8,128)(2,1)} fusion(s32[256]{0:T(256)S(1)} %bitcast.42, bf16[256,256]{1,0:T(8,128)(2,1)S(1)} %reshape.129, bf16[]{:T(256)} %constant.5.clone.1), kind=kCustom, calls=%fused_computation.35 | custom fusion | bytes 196610 | tf_op jit(solution)/shard_map/scatter | solution.py:36
  13.3 5.2 %all-to-all-start.3 = ((bf16[8,48,256]{2,1,0:T(8,128)(2,1)}), bf16[8,48,256]{2,1,0:T(8,128)(2,1)S(1)}, u32[]{:S(2)}, u32[]{:S(2)}) async-start(bf16[8,48,256]{2,1,0:T(8,128)(2,1)} %bitcast.11), calls=%async_computation.3 | async-start | bytes 393216 | tf_op jit(solution)/shard_map/all_to_all | solution.py:58
  18.5 1.0 reshape.121
  19.4 2.1 %scatter_custom_fusion.2 = bf16[384,256]{1,0:T(8,128)(2,1)} fusion(s32[256]{0:T(256)S(1)} %bitcast.43, bf16[256,256]{1,0:T(8,128)(2,1)S(1)} %reshape.121, bf16[]{:T(256)} %constant.5.clone.1), kind=kCustom, calls=%fused_computation.37 | custom fusion | bytes 196610 | tf_op jit(solution)/shard_map/scatter | solution.py:36
  21.5 3.1 %all-to-all-done.3 = bf16[8,48,256]{2,1,0:T(8,128)(2,1)S(1)} async-done(((bf16[8,48,256]{2,1,0:T(8,128)(2,1)}), bf16[8,48,256]{2,1,0:T(8,128)(2,1)S(1)}, u32[]{:S(2)}, u32[]{:S(2)}) %all-to-all-start.3) | async-done | bytes 196640 | tf_op jit(solution)/shard_map/all_to_all | solution.py:58
  24.7 0.0 copy-start
  24.7 0.7 copy-done
  25.4 3.4 %all-to-all-start.2 = ((bf16[8,48,256]{2,1,0:T(8,128)(2,1)}), bf16[8,48,256]{2,1,0:T(8,128)(2,1)S(1)}, u32[]{:S(2)}, u32[]{:S(2)}) async-start(bf16[8,48,256]{2,1,0:T(8,128)(2,1)} %bitcast.9), calls=%async_computation.2 | async-start | bytes 393216 | tf_op jit(solution)/shard_map/all_to_all | solution.py:59
  28.8 0.0 copy-done.3
  28.8 0.1 copy.13
  28.9 0.1 mul.54
  29.0 0.0 copy-done.1
  29.0 1.7 %broadcast_in_dim.21 = f32[128,2,1792]{2,1,0:T(2,128)} broadcast(bf16[128,1792]{1,0:T(8,128)(2,1)S(1)} %copy-done.1), dimensions={0,2} | broadcast | bytes 2293760 | tf_op jit(solution)/shard_map/broadcast_in_dim | solution.py:50
  30.7 2.5 %convert_element_type.50 = f32[256,1792]{1,0:T(8,128)S(1)} reshape(f32[128,2,1792]{2,1,0:T(2,128)} %broadcast_in_dim.21) | data formatting | bytes 3670016 | tf_op jit(solution)/shard_map/convert_element_type | solution.py:50
  33.3 3.2 %scatter_custom_fusion.1 = bf16[384,1792]{1,0:T(8,128)(2,1)} fusion(s32[256]{0:T(256)S(1)} %bitcast.44, f32[256,1792]{1,0:T(8,128)S(1)} %convert_element_type.50, f32[256]{0:T(256)S(1)} %mul.54, bf16[]{:T(256)} %constant.5.clone.1), kind=kCustom, calls=%fused_computation.29 | custom fusion | flops 917504 | bytes 3212290 | tf_op jit(solution)/shard_map/scatter | solution.py:36
  36.5 0.0 copy-start.2
  36.5 0.0 all-to-all-done.2
  36.5 4.3 %all-to-all-start.1 = ((bf16[8,48,1792]{2,1,0:T(8,128)(2,1)}), bf16[8,48,1792]{2,1,0:T(8,128)(2,1)S(1)}, u32[]{:S(2)}, u32[]{:S(2)}) async-start(bf16[8,48,1792]{2,1,0:T(8,128)(2,1)} %bitcast.6), calls=%async_computation.1 | async-start | bytes 2752512 | tf_op jit(solution)/shard_map/all_to_all | solution.py:57
  40.8 0.0 copy-done.2
  40.8 0.5 broadcast_in_dim.20
  41.3 0.3 reshape.105
  41.6 3.2 %scatter_custom_fusion = bf16[384,1792]{1,0:T(8,128)(2,1)} fusion(s32[256]{0:T(256)S(1)} %bitcast.45, bf16[256,1792]{1,0:T(8,128)(2,1)S(1)} %reshape.105, bf16[]{:T(256)} %constant.5.clone.1), kind=kCustom, calls=%fused_computation.33 | custom fusion | bytes 1376258 | tf_op jit(solution)/shard_map/scatter | solution.py:36
  44.8 20.0 %all_gather.7 = bf16[384,1024]{1,0:T(8,128)(2,1)S(1)} all-gather(bf16[384,256]{1,0:T(8,128)(2,1)} %bitcast.40), channel_id=1, replica_groups=mesh['gx'=8,'gy'=4] {'gy'}, dimensions={1}, use_global_device_ids=true | all-gather | bytes 983040 | tf_op jit(solution)/shard_map/all_gather | solution.py:71
  64.8 0.0 all-to-all-done.1
  64.8 4.3 %all-to-all-start = ((bf16[8,48,1792]{2,1,0:T(8,128)(2,1)}), bf16[8,48,1792]{2,1,0:T(8,128)(2,1)}, u32[]{:S(2)}, u32[]{:S(2)}) async-start(bf16[8,48,1792]{2,1,0:T(8,128)(2,1)} %bitcast.4), calls=%async_computation | async-start | bytes 2752512 | tf_op jit(solution)/shard_map/all_to_all | solution.py:56
  69.1 0.0 all-reduce.2.cloned.1.call-start
  69.2 4.5 %fusion.14 = bf16[384,1024]{1,0:T(8,128)(2,1)} fusion(bf16[384,1792]{1,0:T(8,128)(2,1)S(1)} %bitcast.37, bf16[1,1024,1792]{2,1,0:T(8,128)(2,1)} %param.13), kind=kOutput, calls=%fused_computation.28 | convolution fusion | flops 1409679360 | bytes 5832704 | tf_op jit(solution)/shard_map/dot_general | solution.py:65
  73.7 0.0 all-reduce.2.cloned.1.call-update
  73.7 27.0 %all_gather.6 = bf16[384,1024]{1,0:T(8,128)(2,1)S(1)} all-gather(bf16[384,256]{1,0:T(8,128)(2,1)S(1)} %bitcast.39), channel_id=1, replica_groups=mesh['gx'=8,'gy'=4] {'gy'}, dimensions={1}, use_global_device_ids=true | all-gather | bytes 983040 | tf_op jit(solution)/shard_map/all_gather | solution.py:72
  100.8 4.0 %fusion.4 = bf16[1,1024,1792]{2,1,0:T(8,128)(2,1)} fusion(bf16[384,1792]{1,0:T(8,128)(2,1)S(1)} %bitcast.38, bf16[384,1024]{1,0:T(8,128)(2,1)S(1)} %all_gather.6, bf16[384,1024]{1,0:T(8,128)(2,1)S(1)} %all_gather.7), kind=kOutput, calls=%fused_computation.11 | convolution fusion | flops 1414266880 | bytes 6619136 | tf_op jit(solution)/shard_map/dot_general | solution.py:23
  104.8 0.0 all-to-all-done
  104.8 22.1 %all-reduce.2.cloned.1.call-done = bf16[384,1024]{1,0:T(8,128)(2,1)} async-done(((bf16[384,1024]{1,0:T(8,128)(2,1)}), bf16[384,1024]{1,0:T(8,128)(2,1)}) %all-reduce.2.cloned.1.call-update) | async-done | bytes 786448 | tf_op jit(solution)/shard_map/psum | solution.py:69
  126.9 0.0 copy-start.4
  126.9 5.7 %fusion.2 = bf16[1,1792,1024]{2,1,0:T(8,128)(2,1)} fusion(bf16[384,1792]{1,0:T(8,128)(2,1)} %bitcast.5, bf16[384,1024]{1,0:T(8,128)(2,1)S(1)} %all_gather.6, bf16[384,1024]{1,0:T(8,128)(2,1)} %all-reduce.2.cloned.1.call-done, bf16[384,1024]{1,0:T(8,128)(2,1)S(1)} %all_gather.7), kind=kOutput, calls=%fused_computation.9 | convolution fusion | flops 1416232960 | bytes 7405568 | tf_op jit(solution)/shard_map/dot_general | solution.py:23
  132.6 0.0 copy-done.4
  132.6 5.4 %fusion.3 = bf16[1,1792,1024]{2,1,0:T(8,128)(2,1)} fusion(bf16[384,1792]{1,0:T(8,128)(2,1)} %bitcast.5, bf16[384,1024]{1,0:T(8,128)(2,1)S(1)} %copy-done.4, bf16[384,1024]{1,0:T(8,128)(2,1)S(1)} %all_gather.7), kind=kOutput, calls=%fused_computation.10 | convolution fusion | flops 1414266880 | bytes 6619136 | tf_op jit(solution)/shard_map/dot_general | solution.py:23
  (4 shorter events, 0.1 us)
Async XLA Ops:
  7.2 21.6 %copy-start.3 = (f32[128,2]{0,1:T(2,128)S(1)}, f32[128,2]{0,1:T(2,128)}, u32[]{:S(2)}) copy-start(f32[128,2]{0,1:T(2,128)} %param.12) | copy-start | bytes 3076
  7.2 21.8 %copy-start.1 = (bf16[128,1792]{1,0:T(8,128)(2,1)S(1)}, bf16[128,1792]{1,0:T(8,128)(2,1)}, u32[]{:S(2)}) copy-start(bf16[128,1792]{1,0:T(8,128)(2,1)} %param.8) | copy-start | bytes 1376260
  13.3 11.4 %all-to-all-start.3 = ((bf16[8,48,256]{2,1,0:T(8,128)(2,1)}), bf16[8,48,256]{2,1,0:T(8,128)(2,1)S(1)}, u32[]{:S(2)}, u32[]{:S(2)}) async-start(bf16[8,48,256]{2,1,0:T(8,128)(2,1)} %bitcast.11), calls=%async_computation.3 | async-start | bytes 393216 | tf_op jit(solution)/shard_map/all_to_all | solution.py:58
  24.7 0.7 copy-start
  25.4 11.2 %all-to-all-start.2 = ((bf16[8,48,256]{2,1,0:T(8,128)(2,1)}), bf16[8,48,256]{2,1,0:T(8,128)(2,1)S(1)}, u32[]{:S(2)}, u32[]{:S(2)}) async-start(bf16[8,48,256]{2,1,0:T(8,128)(2,1)} %bitcast.9), calls=%async_computation.2 | async-start | bytes 393216 | tf_op jit(solution)/shard_map/all_to_all | solution.py:59
  36.5 4.3 %copy-start.2 = (bf16[128,1792]{1,0:T(8,128)(2,1)S(1)}, bf16[128,1792]{1,0:T(8,128)(2,1)}, u32[]{:S(2)}) copy-start(bf16[128,1792]{1,0:T(8,128)(2,1)} %param.7) | copy-start | bytes 1376260
  36.5 28.3 %all-to-all-start.1 = ((bf16[8,48,1792]{2,1,0:T(8,128)(2,1)}), bf16[8,48,1792]{2,1,0:T(8,128)(2,1)S(1)}, u32[]{:S(2)}, u32[]{:S(2)}) async-start(bf16[8,48,1792]{2,1,0:T(8,128)(2,1)} %bitcast.6), calls=%async_computation.1 | async-start | bytes 2752512 | tf_op jit(solution)/shard_map/all_to_all | solution.py:57
  64.8 40.0 %all-to-all-start = ((bf16[8,48,1792]{2,1,0:T(8,128)(2,1)}), bf16[8,48,1792]{2,1,0:T(8,128)(2,1)}, u32[]{:S(2)}, u32[]{:S(2)}) async-start(bf16[8,48,1792]{2,1,0:T(8,128)(2,1)} %bitcast.4), calls=%async_computation | async-start | bytes 2752512 | tf_op jit(solution)/shard_map/all_to_all | solution.py:56
  69.1 57.8 %all-reduce.2.cloned.1.call-start = ((), (), s32[]{:S(2)}) async-start(), calls=%async_computation.4 | async-start | bytes 1572864 | tf_op jit(solution)/shard_map/psum | solution.py:69
  126.9 5.8 %copy-start.4 = (bf16[384,1024]{1,0:T(8,128)(2,1)S(1)}, bf16[384,1024]{1,0:T(8,128)(2,1)}, u32[]{:S(2)}) copy-start(bf16[384,1024]{1,0:T(8,128)(2,1)} %all-reduce.2.cloned.1.call-done) | copy-start | bytes 2359300
Sparse Core Ops, SparseCore 0:
  73.8 52.9 all-reduce.1
where the time goes:
time: 146 us; the launch traced here: 145 us
  blocking collectives  47.1 us (32%)
  waiting for transfers between devices  25.2 us (17%)
  matrix products  19.7 us (13%)
  starting transfers between devices  17.2 us (12%)
  local copies, waits for them, and re-layouts  16.9 us (12%)
  between operations  14.1 us (10%)
  other arithmetic  4.7 us (3%)
    all_gather x1, blocking collectives, on_device(): lax.all_gather(up_rows, 'gy', axis=1, tiled=True)  27 us
    psum x1, waiting for transfers between devices, on_device(): lax.psum(partial_value.astype(jnp.bfloat16), 'gy').astype(jnp.float32)  22.1 us
    all_gather x1, blocking collectives, on_device(): lax.all_gather(gate_rows, 'gy', axis=1, tiled=True)  20 us
    dot_general x3, matrix products, contract_rows(): lax.dot_general(left, right, (((0,), (0,)), ((), ())), preferred_element_...  15.2 us
    scatter x3, local copies, waits for them, and re-layouts, pack_rows(): jnp.zeros((experts * MOST, values.shape[-1]), values.dtype).at[target]  7.38 us
    all_to_all x1, starting transfers between devices, on_device(): lax.all_to_all(gate_routes, 'gx', split_axis=0, concat_axis=0, tiled=True)  5.2 us
    dot_general x1, matrix products, on_device(): lax.dot_general(rows_grad, weight, (((1,), (1,)), ((), ())), preferred_el...  4.53 us
    all_to_all x1, starting transfers between devices, on_device(): lax.all_to_all(act_routes, 'gx', split_axis=0, concat_axis=0, tiled=True)  4.27 us
  transfers between devices with their start and end apart: 5, of which 2 were waited for; matrix products, arithmetic and copies ran while one was open for 16% of the time, Pallas kernels for 0%

commit v1 on v0

--- a/solution.py
+++ b/solution.py
@@ -66,7 +66,9 @@
         rows_grad, weight, (((1,), (1,)), ((), ())), preferred_element_type=jnp.float32
     )
     rows_act = merge_rows(rows_act)
-    hidden_grad = lax.psum(partial_value.astype(jnp.bfloat16), "gy").astype(jnp.float32)
+    hidden_grad = jnp.sum(lax.all_gather(partial_value.astype(jnp.bfloat16), "gy"), axis=0).astype(
+        jnp.float32
+    )
     gate_full, up_full = (
         lax.all_gather(gate_rows, "gy", axis=1, tiled=True),
         lax.all_gather(up_rows, "gy", axis=1, tiled=True),

time: 146 us -> 159 us (1.089)
  blocking collectives: 47.1 us -> 85.3 us
  waiting for transfers between devices: 25.2 us -> 6.1 us
  starting transfers between devices: 17.2 us -> 10.4 us
  other arithmetic: 4.7 us -> 7.48 us
  matrix products: 19.7 us -> 18 us
    all_to_all x0 -> x1, blocking collectives: none -> 23.8 us  [on_device(): lax.all_to_all(grad_routes, 'gx', split_axis=0, concat_axis=0, tiled=True)]
    psum x1 -> x0, waiting for transfers between devices: 22.1 us -> none  [on_device(): lax.psum(partial_value.astype(jnp.bfloat16), 'gy').astype(jnp.float32)]
    all_gather x1, blocking collectives: 20 us -> 30.6 us  [on_device(): lax.all_gather(gate_rows, 'gy', axis=1, tiled=True)]
    all_to_all x1 -> x0, starting transfers between devices: 4.25 us -> none  [on_device(): lax.all_to_all(grad_routes, 'gx', split_axis=0, concat_axis=0, tiled=True)]
    all_gather x1, blocking collectives: 27 us -> 30.8 us  [on_device(): lax.all_gather(up_rows, 'gy', axis=1, tiled=True)]
    reduce_sum x0 -> x1, other arithmetic: none -> 3.63 us  [on_device(): jnp.sum(lax.all_gather(partial_value.astype(jnp.bfloat16), 'gy'), axis=0)]
    all_to_all x1, waiting for transfers between devices: 0.01 us -> 2.12 us  [on_device(): lax.all_to_all(up_routes, 'gx', split_axis=0, concat_axis=0, tiled=True)]
    all_to_all x1, starting transfers between devices: 5.2 us -> 3.39 us  [on_device(): lax.all_to_all(gate_routes, 'gx', split_axis=0, concat_axis=0, tiled=True)]
  transfers between devices with their start and end apart: 5 -> 4, of which waited for: 2 -> 2; matrix products, arithmetic and copies ran while one was open for 16% -> 10% of each run, Pallas kernels for 0% -> 0%
where the time goes in v1:
time: 159 us
  blocking collectives  85.3 us (54%)
  matrix products  18 us (11%)
  local copies, waits for them, and re-layouts  17.2 us (11%)
  between operations  14.2 us (9%)
  starting transfers between devices  10.4 us (7%)
  other arithmetic  7.48 us (5%)
  waiting for transfers between devices  6.1 us (4%)
    all_gather x1, blocking collectives, on_device(): lax.all_gather(up_rows, 'gy', axis=1, tiled=True)  30.8 us
    all_gather x1, blocking collectives, on_device(): lax.all_gather(gate_rows, 'gy', axis=1, tiled=True)  30.6 us
    all_to_all x1, blocking collectives, on_device(): lax.all_to_all(grad_routes, 'gx', split_axis=0, concat_axis=0, tiled=True)  23.8 us
    dot_general x3, matrix products, contract_rows(): lax.dot_general(left, right, (((0,), (0,)), ((), ())), preferred_element_...  13.4 us
    scatter x3, local copies, waits for them, and re-layouts, pack_rows(): jnp.zeros((experts * MOST, values.shape[-1]), values.dtype).at[target]  7.39 us
    dot_general x1, matrix products, on_device(): lax.dot_general(rows_grad, weight, (((1,), (1,)), ((), ())), preferred_el...  4.57 us
    all_to_all x1, waiting for transfers between devices, on_device(): lax.all_to_all(gate_routes, 'gx', split_axis=0, concat_axis=0, tiled=True)  3.95 us
    reduce_sum x1, other arithmetic, on_device(): jnp.sum(lax.all_gather(partial_value.astype(jnp.bfloat16), 'gy'), axis=0)  3.63 us
  transfers between devices with their start and end apart: 4, of which 2 were waited for; matrix products, arithmetic and copies ran while one was open for 10% of the time, Pallas kernels for 0%

profile of v1, /device:TPU:0, one launch (start us, length us, event | category | flops | bytes accessed | tf_op | source)
XLA Modules:
  0.0 158.5 jit_solution(3381916143588063899)
XLA Ops:
  7.2 0.0 all-gather.3.cloned.1.call-start
  7.2 0.7 broadcast_multiply_fusion
  7.9 0.8 copy.11
  8.7 0.1 eq.29
  8.8 0.1 eq.25
  9.0 0.1 copy.10
  9.1 0.1 mul.52
  9.2 0.6 reduce-window.6
  9.8 0.2 slice_reduce_fusion
  10.1 0.8 copy.13
  10.9 0.1 mul.54
  11.0 2.7 %broadcast_in_dim.21 = f32[128,2,1792]{2,1,0:T(2,128)} broadcast(bf16[128,1792]{1,0:T(8,128)(2,1)} %param.8), dimensions={0,2} | broadcast | bytes 2293760 | tf_op jit(solution)/shard_map/broadcast_in_dim | solution.py:50
  13.7 2.5 %convert_element_type.52 = f32[256,1792]{1,0:T(8,128)S(1)} reshape(f32[128,2,1792]{2,1,0:T(2,128)} %broadcast_in_dim.21) | data formatting | bytes 3670016 | tf_op jit(solution)/shard_map/convert_element_type | solution.py:50
  16.3 0.1 fusion.31
  16.4 2.4 %scatter_custom_fusion.1 = bf16[384,1792]{1,0:T(8,128)(2,1)S(1)} fusion(s32[256]{0:T(256)S(1)} %bitcast.47, f32[256,1792]{1,0:T(8,128)S(1)} %convert_element_type.52, f32[256]{0:T(256)S(1)} %mul.54, bf16[]{:T(256)} %constant.5.clone.1), kind=kCustom, calls=%fused_computation.29 | custom fusion | flops 917504 | bytes 3212290 | tf_op jit(solution)/shard_map/scatter | solution.py:36
  18.8 23.8 %all_to_all.20 = bf16[8,48,1792]{2,1,0:T(8,128)(2,1)S(1)} all-to-all(bf16[8,48,1792]{2,1,0:T(8,128)(2,1)S(1)} %bitcast.38), channel_id=1, replica_groups=mesh['gx'=8,'gy'=4] {'gx'}, dimensions={0} | all-to-all | bytes 2752512 | tf_op jit(solution)/shard_map/all_to_all | solution.py:57
  42.7 0.0 copy-start
  42.7 1.1 copy-done
  43.8 0.0 copy-start.4
  43.8 4.6 %fusion.14 = bf16[384,1024]{1,0:T(8,128)(2,1)} fusion(bf16[384,1792]{1,0:T(8,128)(2,1)S(1)} %bitcast.40, bf16[1,1024,1792]{2,1,0:T(8,128)(2,1)} %param.13), kind=kOutput, calls=%fused_computation.28 | convolution fusion | flops 1409679360 | bytes 5832704 | tf_op jit(solution)/shard_map/dot_general | solution.py:65
  48.3 0.0 copy-start.5
  48.3 0.0 copy-start.3
  48.3 0.0 all-gather.3.cloned.1.call-update
  48.4 0.0 copy-done.4
  48.4 0.1 reshape.129
  48.4 2.1 %scatter_custom_fusion.3 = bf16[384,256]{1,0:T(8,128)(2,1)} fusion(s32[256]{0:T(256)S(1)} %bitcast.48, bf16[256,256]{1,0:T(8,128)(2,1)S(1)} %reshape.129, bf16[]{:T(256)} %constant.5.clone.1), kind=kCustom, calls=%fused_computation.35 | custom fusion | bytes 196610 | tf_op jit(solution)/shard_map/scatter | solution.py:36
  50.5 3.4 %all-to-all-start.3 = ((bf16[8,48,256]{2,1,0:T(8,128)(2,1)}), bf16[8,48,256]{2,1,0:T(8,128)(2,1)S(1)}, u32[]{:S(2)}, u32[]{:S(2)}) async-start(bf16[8,48,256]{2,1,0:T(8,128)(2,1)} %bitcast.12), calls=%async_computation.3 | async-start | bytes 393216 | tf_op jit(solution)/shard_map/all_to_all | solution.py:58
  53.9 0.0 copy-done.5
  53.9 0.1 reshape.121
  54.0 2.1 %scatter_custom_fusion.2 = bf16[384,256]{1,0:T(8,128)(2,1)} fusion(s32[256]{0:T(256)S(1)} %bitcast.49, bf16[256,256]{1,0:T(8,128)(2,1)S(1)} %reshape.121, bf16[]{:T(256)} %constant.5.clone.1), kind=kCustom, calls=%fused_computation.37 | custom fusion | bytes 196610 | tf_op jit(solution)/shard_map/scatter | solution.py:36
  56.1 4.0 %all-to-all-done.3 = bf16[8,48,256]{2,1,0:T(8,128)(2,1)S(1)} async-done(((bf16[8,48,256]{2,1,0:T(8,128)(2,1)}), bf16[8,48,256]{2,1,0:T(8,128)(2,1)S(1)}, u32[]{:S(2)}, u32[]{:S(2)}) %all-to-all-start.3) | async-done | bytes 196640 | tf_op jit(solution)/shard_map/all_to_all | solution.py:58
  60.1 3.4 %all-to-all-start.2 = ((bf16[8,48,256]{2,1,0:T(8,128)(2,1)}), bf16[8,48,256]{2,1,0:T(8,128)(2,1)S(1)}, u32[]{:S(2)}, u32[]{:S(2)}) async-start(bf16[8,48,256]{2,1,0:T(8,128)(2,1)} %bitcast.10), calls=%async_computation.2 | async-start | bytes 393216 | tf_op jit(solution)/shard_map/all_to_all | solution.py:59
  63.5 0.0 copy-done.3
  63.5 0.5 broadcast_in_dim.20
  64.0 0.3 reshape.105
  64.3 3.2 %scatter_custom_fusion = bf16[384,1792]{1,0:T(8,128)(2,1)} fusion(s32[256]{0:T(256)S(1)} %bitcast.50, bf16[256,1792]{1,0:T(8,128)(2,1)S(1)} %reshape.105, bf16[]{:T(256)} %constant.5.clone.1), kind=kCustom, calls=%fused_computation.33 | custom fusion | bytes 1376258 | tf_op jit(solution)/shard_map/scatter | solution.py:36
  67.5 2.1 %all-to-all-done.2 = bf16[8,48,256]{2,1,0:T(8,128)(2,1)S(1)} async-done(((bf16[8,48,256]{2,1,0:T(8,128)(2,1)}), bf16[8,48,256]{2,1,0:T(8,128)(2,1)S(1)}, u32[]{:S(2)}, u32[]{:S(2)}) %all-to-all-start.2) | async-done | bytes 196640 | tf_op jit(solution)/shard_map/all_to_all | solution.py:59
  69.6 3.6 %all-to-all-start = ((bf16[8,48,1792]{2,1,0:T(8,128)(2,1)}), bf16[8,48,1792]{2,1,0:T(8,128)(2,1)S(1)}, u32[]{:S(2)}, u32[]{:S(2)}) async-start(bf16[8,48,1792]{2,1,0:T(8,128)(2,1)} %bitcast.4), calls=%async_computation | async-start | bytes 2752512 | tf_op jit(solution)/shard_map/all_to_all | solution.py:56
  73.2 0.0 copy-start.1
  73.2 30.6 %all_gather.15 = bf16[384,1024]{1,0:T(8,128)(2,1)S(1)} all-gather(bf16[384,256]{1,0:T(8,128)(2,1)S(1)} %bitcast.44), channel_id=1, replica_groups=mesh['gx'=8,'gy'=4] {'gy'}, dimensions={1}, use_global_device_ids=true | all-gather | bytes 983040 | tf_op jit(solution)/shard_map/all_gather | solution.py:73
  103.8 30.8 %all_gather.14 = bf16[384,1024]{1,0:T(8,128)(2,1)S(1)} all-gather(bf16[384,256]{1,0:T(8,128)(2,1)S(1)} %bitcast.45), channel_id=1, replica_groups=mesh['gx'=8,'gy'=4] {'gy'}, dimensions={1}, use_global_device_ids=true | all-gather | bytes 983040 | tf_op jit(solution)/shard_map/all_gather | solution.py:74
  134.6 0.0 copy-done.1
  134.6 4.0 %fusion.4 = bf16[1,1024,1792]{2,1,0:T(8,128)(2,1)} fusion(bf16[384,1792]{1,0:T(8,128)(2,1)S(1)} %bitcast.41, bf16[384,1024]{1,0:T(8,128)(2,1)S(1)} %all_gather.14, bf16[384,1024]{1,0:T(8,128)(2,1)S(1)} %all_gather.15), kind=kOutput, calls=%fused_computation.11 | convolution fusion | flops 1414266880 | bytes 6619136 | tf_op jit(solution)/shard_map/dot_general | solution.py:23
  138.7 3.6 %reduce_sum.25 = bf16[384,1024]{1,0:T(8,128)(2,1)} reduce(bf16[4,384,1024]{2,1,0:T(8,128)(2,1)} %bitcast.39, bf16[]{:T(256)} %constant.5.clone.1), dimensions={0}, to_apply=%region_5.6 | reduce | flops 1179648 | bytes 3932162 | tf_op jit(solution)/shard_map/reduce_sum | solution.py:69
  142.3 0.0 all-to-all-done
  142.3 5.3 %fusion.2 = bf16[1,1792,1024]{2,1,0:T(8,128)(2,1)} fusion(bf16[384,1792]{1,0:T(8,128)(2,1)S(1)} %bitcast.42, bf16[384,1024]{1,0:T(8,128)(2,1)S(1)} %all_gather.14, bf16[384,1024]{1,0:T(8,128)(2,1)} %reduce_sum.25, bf16[384,1024]{1,0:T(8,128)(2,1)S(1)} %all_gather.15), kind=kOutput, calls=%fused_computation.9 | convolution fusion | flops 1416232960 | bytes 7405568 | tf_op jit(solution)/shard_map/dot_general | solution.py:23
  147.6 0.0 copy-done.2
  147.6 4.1 %fusion.3 = bf16[1,1792,1024]{2,1,0:T(8,128)(2,1)} fusion(bf16[384,1792]{1,0:T(8,128)(2,1)S(1)} %bitcast.43, bf16[384,1024]{1,0:T(8,128)(2,1)S(1)} %copy-done.2, bf16[384,1024]{1,0:T(8,128)(2,1)S(1)} %all_gather.15), kind=kOutput, calls=%fused_computation.10 | convolution fusion | flops 1414266880 | bytes 6619136 | tf_op jit(solution)/shard_map/dot_general | solution.py:23
  (6 shorter events, 0.1 us)
Async XLA Ops:
  7.2 131.5 %all-gather.3.cloned.1.call-start = ((), (), s32[]{:S(2)}) async-start(), calls=%async_computation.4 | async-start | bytes 3932160 | tf_op jit(solution)/shard_map/all_gather | solution.py:69
  42.7 1.1 copy-start
  43.8 4.6 %copy-start.4 = (bf16[128,2,256]{2,1,0:T(2,128)(2,1)S(1)}, bf16[128,2,256]{2,1,0:T(2,128)(2,1)}, u32[]{:S(2)}) copy-start(bf16[128,2,256]{2,1,0:T(2,128)(2,1)} %param.9) | copy-start | bytes 393220
  48.3 5.6 %copy-start.5 = (bf16[128,2,256]{2,1,0:T(2,128)(2,1)S(1)}, bf16[128,2,256]{2,1,0:T(2,128)(2,1)}, u32[]{:S(2)}) copy-start(bf16[128,2,256]{2,1,0:T(2,128)(2,1)} %param.10) | copy-start | bytes 393220
  48.3 15.1 %copy-start.3 = (bf16[128,1792]{1,0:T(8,128)(2,1)S(1)}, bf16[128,1792]{1,0:T(8,128)(2,1)}, u32[]{:S(2)}) copy-start(bf16[128,1792]{1,0:T(8,128)(2,1)} %param.7) | copy-start | bytes 1376260
  50.5 9.5 %all-to-all-start.3 = ((bf16[8,48,256]{2,1,0:T(8,128)(2,1)}), bf16[8,48,256]{2,1,0:T(8,128)(2,1)S(1)}, u32[]{:S(2)}, u32[]{:S(2)}) async-start(bf16[8,48,256]{2,1,0:T(8,128)(2,1)} %bitcast.12), calls=%async_computation.3 | async-start | bytes 393216 | tf_op jit(solution)/shard_map/all_to_all | solution.py:58
  60.1 9.5 %all-to-all-start.2 = ((bf16[8,48,256]{2,1,0:T(8,128)(2,1)}), bf16[8,48,256]{2,1,0:T(8,128)(2,1)S(1)}, u32[]{:S(2)}, u32[]{:S(2)}) async-start(bf16[8,48,256]{2,1,0:T(8,128)(2,1)} %bitcast.10), calls=%async_computation.2 | async-start | bytes 393216 | tf_op jit(solution)/shard_map/all_to_all | solution.py:59
  69.6 72.7 %all-to-all-start = ((bf16[8,48,1792]{2,1,0:T(8,128)(2,1)}), bf16[8,48,1792]{2,1,0:T(8,128)(2,1)S(1)}, u32[]{:S(2)}, u32[]{:S(2)}) async-start(bf16[8,48,1792]{2,1,0:T(8,128)(2,1)} %bitcast.4), calls=%async_computation | async-start | bytes 2752512 | tf_op jit(solution)/shard_map/all_to_all | solution.py:56
  73.2 61.4 %copy-start.1 = (bf16[8,48,1792]{2,1,0:T(8,128)(2,1)S(1)}, bf16[8,48,1792]{2,1,0:T(8,128)(2,1)}, u32[]{:S(2)}) copy-start(bf16[8,48,1792]{2,1,0:T(8,128)(2,1)} %copy-done) | copy-start | bytes 4128772
  142.3 5.3 %copy-start.2 = (bf16[384,1024]{1,0:T(8,128)(2,1)S(1)}, bf16[384,1024]{1,0:T(8,128)(2,1)}, u32[]{:S(2)}) copy-start(bf16[384,1024]{1,0:T(8,128)(2,1)} %reduce_sum.25) | copy-start | bytes 2359300
Sparse Core Ops, SparseCore 0:
  48.5 87.7 all-gather.2
